TPU v7x, 32 devices: a whole 2x2x4 slice. The times are simulated.
32 devices in a mesh: member: 4 (over y, x), lon: 8 (over z, core).
Axes of the slice: x: 2, y: 2, z: 4, core: 2. Of those that a mesh axis runs over, the one named last changes fastest.
Arguments:
- fields: bfloat16 [4, 641, 20, 360], P('member', None, None, 'lon'), may hold values from -6 to 6
- weight: bfloat16 [5, 5, 73, 641], replicated, may hold values from -0.046875 to 0.046875
- out_bias: float32 [73], replicated, may hold values from -3 to 3
- observed: float32 [73, 16, 360], P(None, None, 'lon'), may hold values from -6 to 6
- widths: float32 [73], replicated, may hold values from 0.5 to 2
- owner_start: int32 [8, 5], P('lon'), may hold values from 0 to 16, as said below
Outputs:
- out_grad: bfloat16 [4, 73, 16, 360], P('member', None, None, 'lon')
- owned_score: float32 [8, 4, 540], P('lon', 'member')
- weight_grad: float32 [5, 5, 73, 641], replicated
- bias_grad: float32 [73], replicated
Inputs may be any that keep to these rules, and one draw needn't show every extreme that they name: Each row owner_start[l] starts at 0, never falls and ends at 16; owner r of longitude group l holds blocks owner_start[l, r] to owner_start[l, r + 1] - 1, at most 12 of them, and in every group some owner holds exactly 12.
All inputs are finite; a program needn't handle non-finite values.
Results may differ from a plain program's by a relative error of at most 0.0063.
Values may be sent and summed in bfloat16 or wider, within the bound.
No kernel may reach another device: no remote copies, remote signals or barrier semaphores. Data moves between devices by JAX's collectives and lax.ppermute only.
A program may use at most 128 MiB of HBM per device.

v0:
```python
import math
import jax
import jax.numpy as jnp
from jax import lax
from jax.sharding import PartitionSpec as P

BLOCK = 45


def extended(block, sides, width):
    for axis, dim in sides:
        count = lax.axis_size(axis)
        forward = [(i, i + 1) for i in range(count - 1)]
        forward.append((count - 1, 0))
        backward = [(target, source) for source, target in forward]
        low = lax.ppermute(
            lax.slice_in_dim(block, block.shape[dim] - width, None, axis=dim), axis, forward
        )
        high = lax.ppermute(lax.slice_in_dim(block, 0, width, axis=dim), axis, backward)
        block = jnp.concatenate([low, block, high], axis=dim)
    return block


def kernel_terms(values, target, widths):
    members = values.astype(jnp.float32)
    ensemble = members.shape[0]
    inverse = (1.0 / (widths * widths))[:, None]
    spread = members[:, None] - members[None, :]
    kernel_pair = jnp.exp(-0.5 * spread * spread * inverse)
    misfit = members - target[None]
    kernel_obs = jnp.exp(-0.5 * misfit * misfit * inverse)
    per_channel = (
        jnp.sum(kernel_pair, axis=(0, 1)) / (2.0 * ensemble * ensemble)
        - jnp.sum(kernel_obs, axis=0) / ensemble
    )
    scores = jnp.mean(per_channel, axis=0)
    gradient = inverse * (misfit * kernel_obs - jnp.sum(kernel_pair * spread, axis=1) / ensemble)
    return (scores, gradient.astype(jnp.bfloat16))


def tap_stack(gradients, rows_in, padded_width):
    leading = gradients.ndim - 2
    padded = jnp.pad(gradients, [(0, 0)] * leading + [(4, 4), (4, 4)])
    pieces = [
        padded[..., 4 - row_tap : 4 - row_tap + rows_in, 4 - col_tap : 4 - col_tap + padded_width]
        for row_tap in range(5)
        for col_tap in range(5)
    ]
    return jnp.stack(pieces, axis=-4)


def body(fields, weight, out_bias, observed, widths, owner_start):
    local_members, in_chan, rows_in, lon_dev = fields.shape
    out_chan = weight.shape[2]
    rows_out = rows_in - 4
    padded_width = lon_dev + 4
    padded = extended(fields, (("lon", 3),), 2)
    flat_field = padded.reshape(local_members, in_chan, rows_in * padded_width)
    flat_weight = weight.reshape(25 * out_chan, in_chan)
    tap_sums = jnp.einsum(
        "kc,mcp->mkp", flat_weight, flat_field, preferred_element_type=jnp.float32
    )
    tap_sums = tap_sums.reshape(local_members, 5, 5, out_chan, rows_in, padded_width)
    convolved = jnp.broadcast_to(
        out_bias[None, :, None, None], (local_members, out_chan, rows_out, lon_dev)
    )
    for row_tap in range(5):
        for col_tap in range(5):
            convolved = (
                convolved
                + tap_sums[
                    :,
                    row_tap,
                    col_tap,
                    :,
                    row_tap : row_tap + rows_out,
                    col_tap : col_tap + lon_dev,
                ]
            )
    outputs = convolved.astype(jnp.bfloat16)
    owners = lax.axis_size("member")
    own_rank = lax.axis_index("member")
    blocks = rows_out * lon_dev // BLOCK
    capacity = max(2, 3 * blocks // owners)
    starts = owner_start[0]
    slot_index = jnp.arange(capacity, dtype=jnp.int32)
    owned_blocks = starts[1:] - starts[:-1]
    filled = slot_index[None, :] < owned_blocks[:, None]
    global_block = starts[:-1, None] + slot_index[None, :]
    even_blocks = blocks // owners
    sending = outputs.reshape(local_members, out_chan, owners, even_blocks * BLOCK)
    arrived = lax.all_to_all(sending, "member", split_axis=2, concat_axis=0, tiled=True).reshape(
        -1, out_chan, even_blocks * BLOCK
    )
    target = lax.dynamic_slice_in_dim(observed, own_rank * even_blocks, even_blocks, 1)
    target = target.reshape(out_chan, even_blocks * BLOCK)
    scores, gradients = kernel_terms(arrived, target, widths)
    local_grad = lax.all_to_all(
        gradients.reshape(-1, out_chan, 1, even_blocks * BLOCK),
        "member",
        split_axis=0,
        concat_axis=2,
        tiled=True,
    )
    from_self = filled & (global_block // even_blocks == own_rank)
    local_index = jnp.clip(global_block - own_rank * even_blocks, 0, even_blocks - 1)
    parcel = jnp.take(scores.reshape(even_blocks, BLOCK), local_index.reshape(-1), axis=0)
    parcel = jnp.where(from_self[..., None], parcel.reshape(owners, capacity, BLOCK), 0.0)
    gathered = lax.all_to_all(
        parcel.reshape(owners, capacity * BLOCK), "member", split_axis=0, concat_axis=0, tiled=True
    )
    owned_score = jnp.sum(gathered, axis=0).reshape(1, 1, capacity * BLOCK)
    out_grad = local_grad.reshape(local_members, out_chan, rows_out, lon_dev)
    stacked = tap_stack(out_grad, rows_in, padded_width).reshape(
        local_members, 25 * out_chan, rows_in * padded_width
    )
    weight_part = lax.dot_general(
        stacked, flat_field, (((0, 2), (0, 2)), ((), ())), preferred_element_type=jnp.float32
    )
    bias_part = jnp.sum(out_grad.astype(jnp.float32), axis=(0, 2, 3))
    factor = 1.0 / math.sqrt(local_members * owners * rows_out * lon_dev * lax.axis_size("lon"))
    weight_sum, bias_sum = lax.psum((weight_part, bias_part), ("member", "lon"))
    weight_grad = (weight_sum * factor).reshape(5, 5, out_chan, in_chan)
    bias_grad = bias_sum * factor
    return (out_grad, owned_score, weight_grad, bias_grad)


def solution(mesh):
    in_specs = (P("member", None, None, "lon"), P(), P(), P(None, None, "lon"), P(), P("lon", None))
    out_specs = (P("member", None, None, "lon"), P("lon", "member", None), P(), P())
    return jax.shard_map(body, mesh=mesh, in_specs=in_specs, out_specs=out_specs, check_vma=False)
```

profile of v0, /device:TPU:0, one launch (start us, length us, event | category | flops | bytes accessed | tf_op | source)
XLA Modules:
  0.0 309.2 jit_solution(13475572679389987868)
XLA Ops:
  7.2 1.2 fusion.72
  8.4 0.5 collective-permute-start
  8.9 4.1 %collective-permute-start.1 = (bf16[1,641,20,2]{1,3,2,0:T(2,128)(2,1)S(1)}, bf16[1,641,20,2]{1,3,2,0:T(2,128)(2,1)S(1)}, u32[]{:S(2)}, u32[]{:S(2)}) collective-permute-start(bf16[1,641,20,2]{1,3,2,0:T(2,128)(2,1)S(1)} %get-tuple-element.56), channel_id=1, source_target_pairs={{1,0},{2,1},{3,2},{4,3},{5,4},{6,5},{7,6},{0,7},{9,8},{10,9},{11,1... | collective-permute-start | bytes 153848 | tf_op jit(solution)/shard_map/ppermute | solution.py:19
  13.0 0.7 multiply_divide_fusion
  13.7 4.9 %reshape.609 = bf16[1825,641]{1,0:T(8,128)(2,1)} reshape(bf16[5,5,73,641]{3,2,1,0:T(8,128)(2,1)} %param.7) | data formatting | bytes 4679300 | tf_op jit(solution)/shard_map/reshape | solution.py:59
  18.6 2.4 pad_maximum_fusion
  21.0 1.9 reshape.608
  22.9 8.4 %convolution_bitcast_fusion = f32[1,1825,980]{2,1,0:T(8,128)} fusion(bf16[641,980]{0,1:T(8,128)(2,1)} %reshape.608, bf16[1825,641]{1,0:T(8,128)(2,1)} %reshape.609), kind=kOutput, calls=%fused_computation.1 | convolution fusion | flops 2292857088 | bytes 10750010 | tf_op jit(solution)/shard_map/kc,mcp->mkp/dot_general | solution.py:60
  31.2 8.7 %copy.47 = f32[1,1825,980]{1,2,0:T(8,128)} copy(f32[1,1825,980]{2,1,0:T(8,128)} %convolution_bitcast_fusion) | data formatting | bytes 14308000 | tf_op jit(solution)/shard_map/kc,mcp->mkp/transpose | solution.py:60
  39.9 14.5 %reshape.610 = f32[1,5,5,73,20,49]{3,2,1,5,4,0:T(8,128)} reshape(f32[1,1825,980]{1,2,0:T(8,128)} %copy.47) | data formatting | bytes 14308000 | tf_op jit(solution)/shard_map/reshape | solution.py:63
  54.5 22.3 %fusion.70 = (f32[1,1,1,73,16,45]{3,2,1,5,4,0:T(1,128)S(1)}, f32[1,1,1,73,16,45]{3,2,1,5,4,0:T(1,128)S(1)}, f32[1,1,1,73,16,45]{3,2,1,5,4,0:T(1,128)S(1)}, f32[1...) fusion(f32[1,5,5,73,20,49]{3,2,1,5,4,0:T(8,128)} %reshape.610), kind=kLoop, calls=%fused_computation.130 | loop fusion | bytes 7989120 | tf_op jit(solution)/shard_map/slice | solution.py:71
  76.8 9.1 %fusion.71 = (f32[1,1,1,73,16,45]{3,2,1,5,4,0:T(1,128)S(1)}, f32[1,1,1,73,16,45]{3,2,1,5,4,0:T(1,128)S(1)}, f32[1,1,1,73,16,45]{3,2,1,5,4,0:T(1,128)S(1)}, f32[1...) fusion(f32[1,5,5,73,20,49]{3,2,1,5,4,0:T(8,128)} %reshape.610), kind=kLoop, calls=%fused_computation.131 | loop fusion | bytes 2522880 | tf_op jit(solution)/shard_map/slice | solution.py:71
  85.9 3.6 %add_convert_fusion = bf16[1,73,4,180]{1,0,3,2:T(2,128)(2,1)S(1)} fusion(f32[1,73,4,180]{1,0,3,2:T(1,128)S(1)} %bitcast.193, f32[1,73,4,180]{1,0,3,2:T(1,128)S(1)} %bitcast.194, f32[1,73,4,180]{1,0,3,2:T(1,128)S(1)} %bitcast.195, f32[1,73,4,180]{1,0,3,2:T(1,128)S(1)} %bitcast.196, f32[1,73,4,180]{1,0,3,2:T(1,128)S(1)} %bitcast.197, ...), kind=kLoop, calls=%fused_computation.38 | loop fusion | flops 1366560 | bytes 5361412 | tf_op jit(solution)/shard_map/convert_element_type | solution.py:80
  89.5 1.0 copy.48
  90.4 4.2 %all-to-all-start = ((bf16[1,73,4,180]{3,1,0,2:T(8,128)(2,1)}), bf16[1,73,4,180]{3,1,0,2:T(8,128)(2,1)S(1)}, u32[]{:S(2)}, u32[]{:S(2)}) async-start(bf16[1,73,4,180]{3,1,0,2:T(8,128)(2,1)} %copy.48), calls=%async_computation | async-start | bytes 327680 | tf_op jit(solution)/shard_map/all_to_all | solution.py:92
  94.6 0.1 copy.62
  94.8 0.1 reshape.627
  94.9 4.8 %all-to-all-done = bf16[1,73,4,180]{3,1,0,2:T(8,128)(2,1)S(1)} async-done(((bf16[1,73,4,180]{3,1,0,2:T(8,128)(2,1)}), bf16[1,73,4,180]{3,1,0,2:T(8,128)(2,1)S(1)}, u32[]{:S(2)}, u32[]{:S(2)}) %all-to-all-start) | async-done | bytes 105152 | tf_op jit(solution)/shard_map/all_to_all | solution.py:92
  99.7 0.4 fusion.11
  100.2 1.6 fusion.3
  101.9 0.5 fusion.13
  102.4 7.8 %all_to_all.30 = bf16[4,73,1,180]{3,1,2,0:T(8,128)(2,1)S(1)} all-to-all(bf16[4,73,1,180]{3,1,2,0:T(8,128)(2,1)S(1)} %copy.54), channel_id=1, replica_groups=mesh['member'=4,'lon'=8] {'member'}, dimensions={0} | all-to-all | bytes 210240 | tf_op jit(solution)/shard_map/all_to_all | solution.py:98
  110.2 0.6 convert_reduce_fusion
  110.8 0.2 copy.56
  111.2 0.1 fusion.17
  111.3 0.1 fusion.19
  111.4 0.1 fusion.21
  111.5 0.1 fusion.23
  111.7 0.1 fusion.27
  111.8 0.1 fusion.29
  111.9 0.1 fusion.31
  112.0 0.1 fusion.33
  112.1 0.1 fusion.35
  112.2 0.1 fusion.37
  112.3 0.1 fusion.39
  112.4 0.1 fusion.41
  112.5 0.1 fusion.43
  112.7 0.1 fusion.47
  112.8 0.1 fusion.49
  112.9 0.1 fusion.51
  113.0 0.1 fusion.53
  113.2 0.1 fusion.57
  113.3 0.1 fusion.59
  113.4 0.1 fusion.61
  113.5 0.1 fusion.63
  113.6 5.8 %copy.59 = bf16[1,25,73,20,49]{2,1,4,3,0:T(8,128)(2,1)} copy(bf16[1,25,73,20,49]{2,4,3,1,0:T(8,128)(2,1)S(1)} %fusion.63) | data formatting | bytes 7154000 | tf_op jit(solution)/shard_map/stack | solution.py:49
  119.5 13.7 %reshape.613 = bf16[1825,980]{0,1:T(8,128)(2,1)} reshape(bf16[1,25,73,20,49]{2,1,4,3,0:T(8,128)(2,1)} %copy.59) | data formatting | bytes 7154000 | tf_op jit(solution)/shard_map/reshape.9
  133.2 7.4 %fusion.73 = f32[1825,641]{0,1:T(8,128)} fusion(bf16[1825,980]{0,1:T(8,128)(2,1)} %reshape.613, bf16[641,980]{0,1:T(8,128)(2,1)S(1)} %copy-done.2), kind=kOutput, calls=%fused_computation.133 | convolution fusion | flops 2292857088 | bytes 9512660 | tf_op jit(solution)/shard_map/dot_general | solution.py:117
  140.7 0.1 min.9
  140.8 0.1 compare_and_fusion
  141.0 0.1 broadcast_in_dim.41
  141.2 0.1 broadcast_in_dim.43
  141.4 0.1 div.61
  141.4 0.6 gather_fusion
  142.0 0.1 gather.7
  142.2 7.2 %all_to_all.31 = f32[4,1,540]{2,1,0:T(1,128)S(1)} all-to-all(f32[4,1,540]{2,1,0:T(1,128)S(1)} %copy.58), channel_id=1, replica_groups=mesh['member'=4,'lon'=8] {'member'}, dimensions={0} | all-to-all | bytes 17280 | tf_op jit(solution)/shard_map/all_to_all | solution.py:109
  149.4 0.6 reshape.612
  150.0 0.7 copy.61
  150.7 38.1 %psum.15 = f32[73]{0:T(128)S(1)} all-reduce(f32[73]{0:T(128)S(1)} %get-tuple-element.26), channel_id=1, replica_groups=mesh['member'=4,'lon'=8] {'member','lon'}, use_global_device_ids=true, to_apply=%region_7.8 | all-reduce | flops 73 | bytes 584 | tf_op jit(solution)/shard_map/psum | solution.py:122
  188.8 0.5 broadcast_multiply_fusion.3
  189.3 95.6 %all-reduce.3.cloned.1.call-done = f32[1825,641]{0,1:T(8,128)} async-done(((f32[1825,641]{0,1:T(8,128)}), f32[1825,641]{0,1:T(8,128)}) %all-reduce.3.cloned.1.call-update) | async-done | bytes 4679316 | tf_op jit(solution)/shard_map/psum | solution.py:122
  284.9 5.1 %broadcast_multiply_fusion = f32[1825,641]{0,1:T(8,128)} fusion(f32[1825,641]{0,1:T(8,128)} %all-reduce.3.cloned.1.call-done), kind=kLoop, calls=%fused_computation.2 | loop fusion | flops 1169825 | bytes 9358600 | tf_op jit(solution)/shard_map/mul | solution.py:123
  290.0 6.1 %copy.60 = f32[1825,641]{1,0:T(8,128)} copy(f32[1825,641]{0,1:T(8,128)} %broadcast_multiply_fusion) | data formatting | bytes 9358600 | tf_op jit(solution)/shard_map/mul | solution.py:123
  296.1 6.2 %reshape.614 = f32[5,5,73,641]{3,2,1,0:T(8,128)} reshape(f32[1825,641]{1,0:T(8,128)} %copy.60) | data formatting | bytes 9358600 | tf_op jit(solution)/shard_map/reshape | solution.py:123
  (36 shorter events, 0.9 us)
Async XLA Ops:
  7.2 87.4 %copy-start = (f32[73,16,45]{0,1,2:T(8,128)S(1)}, f32[73,16,45]{0,1,2:T(8,128)}, u32[]{:S(2)}) copy-start(f32[73,16,45]{0,1,2:T(8,128)} %param.9) | copy-start | bytes 630724
  8.4 10.2 %collective-permute-start = (bf16[1,641,20,2]{1,3,2,0:T(2,128)(2,1)S(1)}, bf16[1,641,20,2]{1,3,2,0:T(2,128)(2,1)S(1)}, u32[]{:S(2)}, u32[]{:S(2)}) collective-permute-start(bf16[1,641,20,2]{1,3,2,0:T(2,128)(2,1)S(1)} %get-tuple-element.55), channel_id=1, source_target_pairs={{0,1},{1,2},{2,3},{3,4},{4,5},{5,6},{6,7},{7,0},{8,9},{9,10},{10,1... | collective-permute-start | bytes 153848 | tf_op jit(solution)/shard_map/ppermute | solution.py:16
  8.9 9.7 %collective-permute-start.1 = (bf16[1,641,20,2]{1,3,2,0:T(2,128)(2,1)S(1)}, bf16[1,641,20,2]{1,3,2,0:T(2,128)(2,1)S(1)}, u32[]{:S(2)}, u32[]{:S(2)}) collective-permute-start(bf16[1,641,20,2]{1,3,2,0:T(2,128)(2,1)S(1)} %get-tuple-element.56), channel_id=1, source_target_pairs={{1,0},{2,1},{3,2},{4,3},{5,4},{6,5},{7,6},{0,7},{9,8},{10,9},{11,1... | collective-permute-start | bytes 153848 | tf_op jit(solution)/shard_map/ppermute | solution.py:19
  54.5 31.4 %copy-start.3 = (f32[73]{0:T(128)S(1)}, f32[73]{0:T(128)}, u32[]{:S(2)}) copy-start(f32[73]{0:T(128)} %param.8) | copy-start | bytes 880
  90.4 9.3 %all-to-all-start = ((bf16[1,73,4,180]{3,1,0,2:T(8,128)(2,1)}), bf16[1,73,4,180]{3,1,0,2:T(8,128)(2,1)S(1)}, u32[]{:S(2)}, u32[]{:S(2)}) async-start(bf16[1,73,4,180]{3,1,0,2:T(8,128)(2,1)} %copy.48), calls=%async_computation | async-start | bytes 327680 | tf_op jit(solution)/shard_map/all_to_all | solution.py:92
  94.6 190.3 %all-reduce.3.cloned.1.call-start = ((), (), s32[]{:S(2)}) async-start(), calls=%async_computation.3 | async-start | bytes 9953280 | tf_op jit(solution)/shard_map/psum | solution.py:122
  119.5 13.7 %copy-start.2 = (bf16[641,980]{0,1:T(8,128)(2,1)S(1)}, bf16[641,980]{0,1:T(8,128)(2,1)}, u32[]{:S(2)}) copy-start(bf16[641,980]{0,1:T(8,128)(2,1)} %reshape.608) | copy-start | bytes 3769084
  133.2 7.4 %copy-start.4 = (s32[1,5]{1,0:T(1,128)S(1)}, s32[1,5]{1,0:T(1,128)}, u32[]{:S(2)}) copy-start(s32[1,5]{1,0:T(1,128)} %param.11) | copy-start | bytes 64
  290.0 12.3 %copy-start.1 = (f32[73,16,45]{0,1,2:T(8,128)S(1)}, f32[73,16,45]{0,1,2:T(8,128)}, u32[]{:S(2)}) copy-start(f32[73,16,45]{0,1,2:T(8,128)} %param.9) | copy-start | bytes 630724
Sparse Core Ops, SparseCore 0:
  140.7 144.1 all-reduce.2
where the time goes:
time: 311 us; the launch traced here: 309 us
  local copies, waits for them, and re-layouts  101 us (32%)
  waiting for transfers between devices  100 us (32%)
  blocking collectives  53.1 us (17%)
  other arithmetic  15.7 us (5%)
  matrix products  15.7 us (5%)
  between operations  14.3 us (5%)
  starting transfers between devices  8.79 us (3%)
    psum x1, waiting for transfers between devices, body(): weight_sum, bias_sum = lax.psum((weight_part, bias_part), ('member', 'lon'))  95.6 us
    psum x1, blocking collectives, body(): weight_sum, bias_sum = lax.psum((weight_part, bias_part), ('member', 'lon'))  38.1 us
    slice x2, local copies, waits for them, and re-layouts, body(): tap_sums[:, row_tap, col_tap, :, row_tap:row_tap + rows_out, col_tap:col_...  31.4 us
    another operation x2, local copies, waits for them, and re-layouts  15.6 us
    reshape x1, local copies, waits for them, and re-layouts, body(): tap_sums.reshape(local_members, 5, 5, out_chan, rows_in, padded_width)  14.5 us
    transpose x1, local copies, waits for them, and re-layouts, body(): jnp.einsum('kc,mcp->mkp', flat_weight, flat_field, preferred_element_type...  8.69 us
    dot_general x1, matrix products, body(): jnp.einsum('kc,mcp->mkp', flat_weight, flat_field, preferred_element_type...  8.37 us
    all_to_all x1, blocking collectives, body(): lax.all_to_all(gradients.reshape(-1, out_chan, 1, even_blocks * BLOCK), '...  7.82 us
  transfers between devices with their start and end apart: 4, of which 2 were waited for; matrix products, arithmetic and copies ran while one was open for 3% of the time, Pallas kernels for 0%

commit v1 on v0

--- a/solution.py
+++ b/solution.py
@@ -1,10 +1,19 @@
+import functools
 import math
 import jax
 import jax.numpy as jnp
 from jax import lax
 from jax.sharding import PartitionSpec as P
+from jax.lax import psum
 
 BLOCK = 45
+
+
+def push_the_sites(vec, peer_axis, a_name):
+    return psum(psum(vec, peer_axis), a_name)
+
+
+attach_tables = functools.partial(push_the_sites, peer_axis="lon", a_name="member")
 
 
 def extended(block, sides, width):
@@ -119,7 +128,7 @@
     )
     bias_part = jnp.sum(out_grad.astype(jnp.float32), axis=(0, 2, 3))
     factor = 1.0 / math.sqrt(local_members * owners * rows_out * lon_dev * lax.axis_size("lon"))
-    weight_sum, bias_sum = lax.psum((weight_part, bias_part), ("member", "lon"))
+    weight_sum, bias_sum = attach_tables((weight_part, bias_part))
     weight_grad = (weight_sum * factor).reshape(5, 5, out_chan, in_chan)
     bias_grad = bias_sum * factor
     return (out_grad, owned_score, weight_grad, bias_grad)

time: 311 us -> 396 us (1.27)
  waiting for transfers between devices: 100 us -> 200 us
  blocking collectives: 53.1 us -> 38.5 us
    psum x1 -> x2, waiting for transfers between devices: 95.6 us -> 195 us  [push_the_sites(): return psum(psum(vec, peer_axis), a_name)]
    psum x1 -> x2, blocking collectives: 38.1 us -> 22.5 us  [push_the_sites(): return psum(psum(vec, peer_axis), a_name)]
  transfers between devices with their start and end apart: 4 -> 5, of which waited for: 2 -> 3; matrix products, arithmetic and copies ran while one was open for 3% -> 2% of each run, Pallas kernels for 0% -> 0%
where the time goes in v1:
time: 396 us; the launch traced here: 394 us
  waiting for transfers between devices  200 us (51%)
  local copies, waits for them, and re-layouts  101 us (26%)
  blocking collectives  38.5 us (10%)
  other arithmetic  15.7 us (4%)
  matrix products  15.7 us (4%)
  between operations  14.3 us (4%)
  starting transfers between devices  8.83 us (2%)
    psum x2, waiting for transfers between devices, push_the_sites(): return psum(psum(vec, peer_axis), a_name)  195 us
    slice x2, local copies, waits for them, and re-layouts, body(): tap_sums[:, row_tap, col_tap, :, row_tap:row_tap + rows_out, col_tap:col_...  31.4 us
    psum x2, blocking collectives, push_the_sites(): return psum(psum(vec, peer_axis), a_name)  22.5 us
    another operation x2, local copies, waits for them, and re-layouts  15.6 us
    reshape x1, local copies, waits for them, and re-layouts, body(): tap_sums.reshape(local_members, 5, 5, out_chan, rows_in, padded_width)  14.5 us
    transpose x1, local copies, waits for them, and re-layouts, body(): jnp.einsum('kc,mcp->mkp', flat_weight, flat_field, preferred_element_type...  8.69 us
    dot_general x1, matrix products, body(): jnp.einsum('kc,mcp->mkp', flat_weight, flat_field, preferred_element_type...  8.37 us
    all_to_all x1, blocking collectives, body(): lax.all_to_all(parcel.reshape(owners, capacity * BLOCK), 'member', split_...  8.15 us
  transfers between devices with their start and end apart: 5, of which 3 were waited for; matrix products, arithmetic and copies ran while one was open for 2% of the time, Pallas kernels for 0%

profile of v1, /device:TPU:0, one launch (start us, length us, event | category | flops | bytes accessed | tf_op | source)
XLA Modules:
  0.0 394.2 jit_solution(2468471615739666669)
XLA Ops:
  7.2 1.2 fusion.72
  8.4 0.5 collective-permute-start
  8.9 4.1 %collective-permute-start.1 = (bf16[1,641,20,2]{1,3,2,0:T(2,128)(2,1)S(1)}, bf16[1,641,20,2]{1,3,2,0:T(2,128)(2,1)S(1)}, u32[]{:S(2)}, u32[]{:S(2)}) collective-permute-start(bf16[1,641,20,2]{1,3,2,0:T(2,128)(2,1)S(1)} %get-tuple-element.56), channel_id=1, source_target_pairs={{1,0},{2,1},{3,2},{4,3},{5,4},{6,5},{7,6},{0,7},{9,8},{10,9},{11,1... | collective-permute-start | bytes 153848 | tf_op jit(solution)/shard_map/ppermute | solution.py:28
  13.0 0.7 multiply_divide_fusion
  13.7 4.9 %reshape.609 = bf16[1825,641]{1,0:T(8,128)(2,1)} reshape(bf16[5,5,73,641]{3,2,1,0:T(8,128)(2,1)} %param.7) | data formatting | bytes 4679300 | tf_op jit(solution)/shard_map/reshape | solution.py:68
  18.6 2.4 pad_maximum_fusion
  21.0 1.9 reshape.608
  22.9 8.4 %convolution_bitcast_fusion = f32[1,1825,980]{2,1,0:T(8,128)} fusion(bf16[641,980]{0,1:T(8,128)(2,1)} %reshape.608, bf16[1825,641]{1,0:T(8,128)(2,1)} %reshape.609), kind=kOutput, calls=%fused_computation.1 | convolution fusion | flops 2292857088 | bytes 10750010 | tf_op jit(solution)/shard_map/kc,mcp->mkp/dot_general | solution.py:69
  31.2 8.7 %copy.47 = f32[1,1825,980]{1,2,0:T(8,128)} copy(f32[1,1825,980]{2,1,0:T(8,128)} %convolution_bitcast_fusion) | data formatting | bytes 14308000 | tf_op jit(solution)/shard_map/kc,mcp->mkp/transpose | solution.py:69
  39.9 14.5 %reshape.610 = f32[1,5,5,73,20,49]{3,2,1,5,4,0:T(8,128)} reshape(f32[1,1825,980]{1,2,0:T(8,128)} %copy.47) | data formatting | bytes 14308000 | tf_op jit(solution)/shard_map/reshape | solution.py:72
  54.5 22.3 %fusion.70 = (f32[1,1,1,73,16,45]{3,2,1,5,4,0:T(1,128)S(1)}, f32[1,1,1,73,16,45]{3,2,1,5,4,0:T(1,128)S(1)}, f32[1,1,1,73,16,45]{3,2,1,5,4,0:T(1,128)S(1)}, f32[1...) fusion(f32[1,5,5,73,20,49]{3,2,1,5,4,0:T(8,128)} %reshape.610), kind=kLoop, calls=%fused_computation.130 | loop fusion | bytes 7989120 | tf_op jit(solution)/shard_map/slice | solution.py:80
  76.8 9.1 %fusion.71 = (f32[1,1,1,73,16,45]{3,2,1,5,4,0:T(1,128)S(1)}, f32[1,1,1,73,16,45]{3,2,1,5,4,0:T(1,128)S(1)}, f32[1,1,1,73,16,45]{3,2,1,5,4,0:T(1,128)S(1)}, f32[1...) fusion(f32[1,5,5,73,20,49]{3,2,1,5,4,0:T(8,128)} %reshape.610), kind=kLoop, calls=%fused_computation.131 | loop fusion | bytes 2522880 | tf_op jit(solution)/shard_map/slice | solution.py:80
  85.9 3.6 add_convert_fusion
  89.5 1.0 copy.48
  90.4 4.2 %all-to-all-start = ((bf16[1,73,4,180]{3,1,0,2:T(8,128)(2,1)}), bf16[1,73,4,180]{3,1,0,2:T(8,128)(2,1)S(1)}, u32[]{:S(2)}, u32[]{:S(2)}) async-start(bf16[1,73,4,180]{3,1,0,2:T(8,128)(2,1)} %copy.48), calls=%async_computation | async-start | bytes 327680 | tf_op jit(solution)/shard_map/all_to_all | solution.py:101
  94.6 0.1 copy.62
  94.8 0.1 reshape.627
  94.9 4.8 %all-to-all-done = bf16[1,73,4,180]{3,1,0,2:T(8,128)(2,1)S(1)} async-done(((bf16[1,73,4,180]{3,1,0,2:T(8,128)(2,1)}), bf16[1,73,4,180]{3,1,0,2:T(8,128)(2,1)S(1)}, u32[]{:S(2)}, u32[]{:S(2)}) %all-to-all-start) | async-done | bytes 105152 | tf_op jit(solution)/shard_map/all_to_all | solution.py:101
  99.7 0.4 fusion.11
  100.2 1.6 fusion.3
  101.9 0.5 fusion.13
  102.4 7.8 %all_to_all.30 = bf16[4,73,1,180]{3,1,2,0:T(8,128)(2,1)S(1)} all-to-all(bf16[4,73,1,180]{3,1,2,0:T(8,128)(2,1)S(1)} %copy.54), channel_id=1, replica_groups=mesh['member'=4,'lon'=8] {'member'}, dimensions={0} | all-to-all | bytes 210240 | tf_op jit(solution)/shard_map/all_to_all | solution.py:107
  110.2 0.6 convert_reduce_fusion
  110.8 0.2 copy.56
  111.2 0.1 fusion.17
  111.3 0.1 fusion.19
  111.4 0.1 fusion.21
  111.5 0.1 fusion.23
  111.7 0.1 fusion.27
  111.8 0.1 fusion.29
  111.9 0.1 fusion.31
  112.0 0.1 fusion.33
  112.2 0.1 fusion.37
  112.3 0.1 fusion.39
  112.4 0.1 fusion.41
  112.5 0.1 fusion.43
  112.7 0.1 fusion.47
  112.8 0.1 fusion.49
  112.9 0.1 fusion.51
  113.0 0.1 fusion.53
  113.2 0.1 fusion.57
  113.3 0.1 fusion.59
  113.4 0.1 fusion.61
  113.5 0.1 fusion.63
  113.6 5.8 %copy.59 = bf16[1,25,73,20,49]{2,1,4,3,0:T(8,128)(2,1)} copy(bf16[1,25,73,20,49]{2,4,3,1,0:T(8,128)(2,1)S(1)} %fusion.63) | data formatting | bytes 7154000 | tf_op jit(solution)/shard_map/stack | solution.py:58
  119.5 13.7 %reshape.613 = bf16[1825,980]{0,1:T(8,128)(2,1)} reshape(bf16[1,25,73,20,49]{2,1,4,3,0:T(8,128)(2,1)} %copy.59) | data formatting | bytes 7154000 | tf_op jit(solution)/shard_map/reshape.9
  133.2 7.3 %fusion.73 = f32[1825,641]{0,1:T(8,128)} fusion(bf16[1825,980]{0,1:T(8,128)(2,1)} %reshape.613, bf16[641,980]{0,1:T(8,128)(2,1)S(1)} %copy-done.2), kind=kOutput, calls=%fused_computation.133 | convolution fusion | flops 2292857088 | bytes 9512660 | tf_op jit(solution)/shard_map/dot_general | solution.py:126
  140.6 109.0 %all-reduce.4.cloned.1.call-done = f32[1825,641]{0,1:T(8,128)} async-done(((f32[1825,641]{0,1:T(8,128)}), f32[1825,641]{0,1:T(8,128)}) %all-reduce.4.cloned.1.call-update) | async-done | bytes 4679316 | tf_op jit(solution)/shard_map/psum | solution.py:13
  249.8 0.1 min.9
  250.1 0.1 broadcast_in_dim.41
  250.3 0.1 broadcast_in_dim.43
  250.5 0.1 div.61
  250.5 0.6 gather_fusion
  251.1 0.1 gather.7
  251.3 8.1 %all_to_all.31 = f32[4,1,540]{2,1,0:T(1,128)S(1)} all-to-all(f32[4,1,540]{2,1,0:T(1,128)S(1)} %copy.58), channel_id=1, replica_groups=mesh['member'=4,'lon'=8] {'member'}, dimensions={0} | all-to-all | bytes 17280 | tf_op jit(solution)/shard_map/all_to_all | solution.py:118
  259.4 0.6 reshape.612
  260.0 0.7 copy.61
  260.7 13.9 %psum.30 = f32[73]{0:T(128)S(1)} all-reduce(f32[73]{0:T(128)S(1)} %get-tuple-element.26), channel_id=1, replica_groups=mesh['member'=4,'lon'=8] {'lon'}, use_global_device_ids=true, to_apply=%region_8.9 | all-reduce | flops 73 | bytes 584 | tf_op jit(solution)/shard_map/psum | solution.py:13
  274.7 8.6 %psum.31 = f32[73]{0:T(128)S(1)} all-reduce(f32[73]{0:T(128)S(1)} %psum.30), channel_id=1, replica_groups=mesh['member'=4,'lon'=8] {'member'}, use_global_device_ids=true, to_apply=%region_9.10 | all-reduce | flops 73 | bytes 584 | tf_op jit(solution)/shard_map/psum | solution.py:13
  283.2 0.5 broadcast_multiply_fusion.3
  283.8 86.1 %all-reduce.6.cloned.1.call-done = f32[1825,641]{0,1:T(8,128)} async-done(((f32[1825,641]{0,1:T(8,128)}), f32[1825,641]{0,1:T(8,128)}) %all-reduce.6.cloned.1.call-update) | async-done | bytes 4679316 | tf_op jit(solution)/shard_map/psum | solution.py:13
  369.9 5.1 %broadcast_multiply_fusion = f32[1825,641]{0,1:T(8,128)} fusion(f32[1825,641]{0,1:T(8,128)} %all-reduce.6.cloned.1.call-done), kind=kLoop, calls=%fused_computation.2 | loop fusion | flops 1169825 | bytes 9358600 | tf_op jit(solution)/shard_map/mul | solution.py:132
  375.0 6.1 %copy.60 = f32[1825,641]{1,0:T(8,128)} copy(f32[1825,641]{0,1:T(8,128)} %broadcast_multiply_fusion) | data formatting | bytes 9358600 | tf_op jit(solution)/shard_map/mul | solution.py:132
  381.1 6.2 %reshape.614 = f32[5,5,73,641]{3,2,1,0:T(8,128)} reshape(f32[1825,641]{1,0:T(8,128)} %copy.60) | data formatting | bytes 9358600 | tf_op jit(solution)/shard_map/reshape | solution.py:132
  (40 shorter events, 1.2 us)
Async XLA Ops:
  7.2 87.4 %copy-start = (f32[73,16,45]{0,1,2:T(8,128)S(1)}, f32[73,16,45]{0,1,2:T(8,128)}, u32[]{:S(2)}) copy-start(f32[73,16,45]{0,1,2:T(8,128)} %param.9) | copy-start | bytes 630724
  8.4 10.2 %collective-permute-start = (bf16[1,641,20,2]{1,3,2,0:T(2,128)(2,1)S(1)}, bf16[1,641,20,2]{1,3,2,0:T(2,128)(2,1)S(1)}, u32[]{:S(2)}, u32[]{:S(2)}) collective-permute-start(bf16[1,641,20,2]{1,3,2,0:T(2,128)(2,1)S(1)} %get-tuple-element.55), channel_id=1, source_target_pairs={{0,1},{1,2},{2,3},{3,4},{4,5},{5,6},{6,7},{7,0},{8,9},{9,10},{10,1... | collective-permute-start | bytes 153848 | tf_op jit(solution)/shard_map/ppermute | solution.py:25
  8.9 9.7 %collective-permute-start.1 = (bf16[1,641,20,2]{1,3,2,0:T(2,128)(2,1)S(1)}, bf16[1,641,20,2]{1,3,2,0:T(2,128)(2,1)S(1)}, u32[]{:S(2)}, u32[]{:S(2)}) collective-permute-start(bf16[1,641,20,2]{1,3,2,0:T(2,128)(2,1)S(1)} %get-tuple-element.56), channel_id=1, source_target_pairs={{1,0},{2,1},{3,2},{4,3},{5,4},{6,5},{7,6},{0,7},{9,8},{10,9},{11,1... | collective-permute-start | bytes 153848 | tf_op jit(solution)/shard_map/ppermute | solution.py:28
  54.5 31.4 %copy-start.3 = (f32[73]{0:T(128)S(1)}, f32[73]{0:T(128)}, u32[]{:S(2)}) copy-start(f32[73]{0:T(128)} %param.8) | copy-start | bytes 880
  90.4 9.3 %all-to-all-start = ((bf16[1,73,4,180]{3,1,0,2:T(8,128)(2,1)}), bf16[1,73,4,180]{3,1,0,2:T(8,128)(2,1)S(1)}, u32[]{:S(2)}, u32[]{:S(2)}) async-start(bf16[1,73,4,180]{3,1,0,2:T(8,128)(2,1)} %copy.48), calls=%async_computation | async-start | bytes 327680 | tf_op jit(solution)/shard_map/all_to_all | solution.py:101
  94.6 155.1 %all-reduce.4.cloned.1.call-start = ((), (), s32[]{:S(2)}) async-start(), calls=%async_computation.3 | async-start | bytes 9953280 | tf_op jit(solution)/shard_map/psum | solution.py:13
  119.5 13.7 %copy-start.2 = (bf16[641,980]{0,1:T(8,128)(2,1)S(1)}, bf16[641,980]{0,1:T(8,128)(2,1)}, u32[]{:S(2)}) copy-start(bf16[641,980]{0,1:T(8,128)(2,1)} %reshape.608) | copy-start | bytes 3769084
  140.5 109.1 %copy-start.4 = (s32[1,5]{1,0:T(1,128)S(1)}, s32[1,5]{1,0:T(1,128)}, u32[]{:S(2)}) copy-start(s32[1,5]{1,0:T(1,128)} %param.11) | copy-start | bytes 64
  140.6 229.3 %all-reduce.6.cloned.1.call-start = ((), (), s32[]{:S(2)}) async-start(), calls=%async_computation.4 | async-start | bytes 9953280 | tf_op jit(solution)/shard_map/psum | solution.py:13
  375.0 12.3 %copy-start.1 = (f32[73,16,45]{0,1,2:T(8,128)S(1)}, f32[73,16,45]{0,1,2:T(8,128)}, u32[]{:S(2)}) copy-start(f32[73,16,45]{0,1,2:T(8,128)} %param.9) | copy-start | bytes 630724
Sparse Core Ops, SparseCore 0:
  140.7 108.9 all-reduce.3
  253.0 116.8 all-reduce.5
